TPU v7x, 256 devices: a whole 4x4x8 slice. The times are simulated.
256 devices in a mesh: ctx: 8 (over z_lo, core), ep: 32 (over y, x, z_hi).
Axes of the slice: x: 4, y: 4, z: 8 (z_hi: 2, z_lo: 4; z = z_hi * 4 + z_lo), core: 2. Of those that a mesh axis runs over, the one named last changes fastest.
Arguments:
- queries: bfloat16 [32768, 2048], P(('ctx', 'ep')), may hold values from -40 to 40
- keys: bfloat16 [32768, 256], P(('ctx', 'ep')), may hold values from -40 to 40
- values: bfloat16 [32768, 256], P(('ctx', 'ep')), may hold values from -6 to 6
- prior_out: bfloat16 [32768, 2048], P(('ctx', 'ep')), may hold values from -6 to 6
- prior_lse: float32 [32768, 16], P(('ctx', 'ep')), may hold values from 4 to 8
- residual: bfloat16 [32768, 2048], P(('ctx', 'ep')), may hold values from -40 to 40
- out_proj: bfloat16 [2048, 2048], P(('ctx', 'ep')), may hold values from -0.5 to 0.5
- norm_gain: float32 [2048], replicated, may hold values from 0.5 to 1.5
- expert_in: bfloat16 [32, 2048, 1536], P('ep'), may hold values from -0.125 to 0.125
- expert_out: bfloat16 [32, 768, 2048], P('ep'), may hold values from -0.21875 to 0.21875
- expert_ids: int32 [32768, 8], P(('ctx', 'ep')), may hold values from 0 to 31, as said below
- route_weight: float32 [32768, 8], P(('ctx', 'ep')), may hold values from 0.05 to 0.6
Outputs:
- layer_out: bfloat16 [32768, 2048], P(('ctx', 'ep'))
- attended: bfloat16 [32768, 2048], P(('ctx', 'ep'))
Inputs may be any that keep to these rules, and one draw needn't show every extreme that they name: `expert_ids`: each row names 8 different experts. In the rows of one device no expert is named more than 40 times, and one expert is named exactly 40 times in the rows of every device.
All inputs are finite; a program needn't handle non-finite values.
Results may differ from a plain program's by a relative error of at most 0.0061.
Values may be sent and summed in bfloat16 or wider, within the bound.
A program may use at most 128 MiB of HBM per device.

v0:
```python
import math
import jax
import jax.numpy as jnp
from jax import lax
from jax.sharding import PartitionSpec as P

HEADS = 16
KVH = 2
HD = 128
GROUP = 8


def passed_along(shard, axis, by):
    devices = lax.axis_size(axis)
    return lax.ppermute(shard, axis, [(i, (i + by) % devices) for i in range(devices)])


def run_expert(inputs, weight_in, weight_out, hidden_units):
    flat_in = inputs.reshape(-1, inputs.shape[-1])
    gate_up = jnp.dot(flat_in, weight_in, preferred_element_type=jnp.float32)
    activated = (jax.nn.silu(gate_up[:, :hidden_units]) * gate_up[:, hidden_units:]).astype(
        jnp.bfloat16
    )
    replies = jnp.dot(activated, weight_out, preferred_element_type=jnp.float32).astype(
        jnp.bfloat16
    )
    return replies.reshape(inputs.shape[:-1] + (weight_out.shape[-1],))


def shards(
    queries,
    keys,
    values,
    prior_out,
    prior_lse,
    residual,
    out_proj,
    norm_gain,
    expert_in,
    expert_out,
    expert_ids,
    route_weight,
):
    local_rows = queries.shape[0]
    ctx_count = lax.axis_size("ctx")
    ctx_here = lax.axis_index("ctx")
    ep_count = lax.axis_size("ep")
    reach_steps = min(2, ctx_count - 1)
    kv_pair = jnp.stack([keys, values])
    arrived = []
    current = kv_pair
    for stride in range(reach_steps):
        current = passed_along(current, "ctx", 1)
        arrived.append(current)
    window = jnp.concatenate(arrived, axis=1)
    width_kv = window.shape[1]
    key_win = window[0].reshape(width_kv, KVH, HD)
    value_win = window[1].reshape(width_kv, KVH, HD)
    query_blk = queries.reshape(local_rows, KVH, GROUP, HD)
    scores = jnp.einsum(
        "ighd,jgd->ghij", query_blk, key_win, preferred_element_type=jnp.float32
    ) / math.sqrt(HD)
    positions = jnp.arange(width_kv, dtype=jnp.int32)
    key_local = positions % local_rows
    key_ctx = (ctx_here - (positions // local_rows + 1)) % ctx_count
    query_local = jnp.arange(local_rows, dtype=jnp.int32)[:, None]
    visible = (key_local[None, :] < query_local) | (key_local[None, :] == query_local) & (
        key_ctx[None, :] <= ctx_here
    )
    scores = jnp.where(visible, scores, -jnp.inf)
    lse_prior = prior_lse.reshape(local_rows, KVH, GROUP).transpose(1, 2, 0)
    top_score = jnp.maximum(lse_prior, jnp.max(scores, axis=-1))
    weights = jnp.exp(scores - top_score[..., None])
    prior_weight = jnp.exp(lse_prior - top_score)
    totals = prior_weight + jnp.sum(weights, axis=-1)
    gathered = jnp.einsum(
        "ghij,jgd->ighd",
        weights.astype(jnp.bfloat16),
        value_win,
        preferred_element_type=jnp.float32,
    )
    prior_part = (
        prior_out.reshape(local_rows, KVH, GROUP, HD).astype(jnp.float32)
        * prior_weight.transpose(2, 0, 1)[..., None]
    )
    attended = ((prior_part + gathered) / totals.transpose(2, 0, 1)[..., None]).astype(jnp.bfloat16)
    attended = attended.reshape(local_rows, HEADS * HD)
    model_width = out_proj.shape[1]
    projected = jnp.dot(
        attended,
        lax.all_gather(out_proj, ("ctx", "ep"), axis=0, tiled=True),
        preferred_element_type=jnp.float32,
    )
    mixed_state = (residual.astype(jnp.float32) + projected).astype(jnp.bfloat16)
    state_f = lax.optimization_barrier(mixed_state).astype(jnp.float32)
    normed = (
        state_f * lax.rsqrt(jnp.mean(state_f * state_f, axis=-1, keepdims=True) + 1e-06) * norm_gain
    ).astype(jnp.bfloat16)
    experts_all = ep_count * expert_in.shape[0]
    top_count = expert_ids.shape[1]
    capacity = max(
        local_rows // 4, top_count * ((local_rows + experts_all - 2) // (experts_all - 1))
    )
    flat_ids = expert_ids.reshape(-1)
    one_hot = (flat_ids[:, None] == jnp.arange(experts_all, dtype=jnp.int32)[None, :]).astype(
        jnp.int32
    )
    earlier = jnp.cumsum(one_hot, axis=0) - one_hot
    slot_ids = flat_ids * capacity + jnp.sum(earlier * one_hot, axis=1)
    outgoing = jnp.zeros((experts_all * capacity, model_width), jnp.bfloat16)
    outgoing = (
        outgoing.at[slot_ids]
        .set(jnp.repeat(normed, top_count, axis=0))
        .reshape(experts_all, capacity, model_width)
    )
    weight_in = expert_in[0]
    weight_out = expert_out[0]
    hidden_units = weight_out.shape[0]
    replies = run_expert(
        lax.all_to_all(outgoing, "ep", split_axis=0, concat_axis=0, tiled=True),
        weight_in,
        weight_out,
        hidden_units,
    )
    returned = lax.all_to_all(replies, "ep", split_axis=0, concat_axis=0, tiled=True)
    picked = returned.reshape(experts_all * capacity, model_width)[slot_ids].reshape(
        local_rows, top_count, model_width
    )
    combined = jnp.sum(route_weight[:, :, None] * picked.astype(jnp.float32), axis=1)
    layer_out = (state_f + combined).astype(jnp.bfloat16)
    return (layer_out, attended)


def solution(mesh):
    return jax.shard_map(
        shards,
        mesh=mesh,
        in_specs=(
            P(("ctx", "ep"), None),
            P(("ctx", "ep"), None),
            P(("ctx", "ep"), None),
            P(("ctx", "ep"), None),
            P(("ctx", "ep"), None),
            P(("ctx", "ep"), None),
            P(("ctx", "ep"), None),
            P(),
            P("ep", None, None),
            P("ep", None, None),
            P(("ctx", "ep"), None),
            P(("ctx", "ep"), None),
        ),
        out_specs=(P(("ctx", "ep"), None), P(("ctx", "ep"), None)),
        check_vma=False,
    )
```

profile of v0, /device:TPU:105, one launch (start us, length us, event | category | flops | bytes accessed | tf_op | source)
XLA Modules:
  0.0 1047.9 jit_solution(17184374419318209309)
XLA Ops:
  7.2 0.7 all-gather.2.cloned.1.call-update
  7.9 1.2 copy.21
  9.1 1.0 copy.22
  10.0 0.7 pad_maximum_fusion
  10.7 0.8 copy.28
  11.6 9.0 reduce-window.6
  20.7 0.1 copy.30
  21.0 0.1 fusion.27
  21.3 0.7 broadcast_multiply_fusion
  22.0 0.1 copy.27
  22.4 2.0 copy.38
  24.4 2.3 copy.20
  26.7 1.0 constant_dynamic-update-slice_fusion.1
  27.8 1.6 fusion.39
  29.4 0.3 fusion.12
  29.7 1.3 fusion.16
  31.0 678.4 %all-gather.2.cloned.1.call-done = bf16[2048,2048]{1,0:T(8,128)(2,1)} async-done(((bf16[8,2048]{1,0:T(8,128)(2,1)}), bf16[2048,2048]{1,0:T(8,128)(2,1)}) %all-gather.2.cloned.1.call-update) | async-done | bytes 8388624 | tf_op jit(solution)/shard_map/all_gather | solution.py:91
  709.4 4.9 fusion.8
  714.3 0.2 fusion.17
  714.5 0.6 copy-done.1
  715.1 1.0 fusion.19
  716.1 10.1 scatter_custom_fusion
  726.2 146.0 %all_to_all.10 = bf16[32,40,2048]{2,1,0:T(8,128)(2,1)S(1)} all-to-all(bf16[32,40,2048]{2,1,0:T(8,128)(2,1)} %bitcast.79), channel_id=1, replica_groups=mesh['ctx'=8,'ep'=32] {'ep'}, dimensions={0} | all-to-all | bytes 10485760 | tf_op jit(solution)/shard_map/all_to_all | solution.py:120
  872.2 10.5 %fusion.1 = f32[1280,1536]{1,0:T(8,128)S(1)} fusion(bf16[1280,2048]{1,0:T(8,128)(2,1)S(1)} %bitcast.81, bf16[1,2048,1536]{2,1,0:T(8,128)(2,1)} %param.20), kind=kOutput, calls=%fused_computation.5 | convolution fusion | flops 8053063680 | bytes 19398656 | tf_op jit(solution)/shard_map/dot_general | solution.py:20
  882.7 6.1 convolution_convert_fusion
  888.8 8.2 all-to-all-start.1
  897.0 0.1 copy.26
  897.1 2.0 copy.32
  899.2 122.4 %all-to-all-done.1 = bf16[32,40,2048]{2,1,0:T(8,128)(2,1)} async-done(((bf16[32,40,2048]{2,1,0:T(8,128)(2,1)}), bf16[32,40,2048]{2,1,0:T(8,128)(2,1)}, u32[]{:S(2)}, u32[]{:S(2)}) %all-to-all-start.1) | async-done | bytes 5242912 | tf_op jit(solution)/shard_map/all_to_all | solution.py:125
  1021.6 12.0 %gather_fusion = bf16[1024,2048]{1,0:T(8,128)(2,1)} fusion(bf16[1280,2048]{1,0:T(8,128)(2,1)} %bitcast.25, s32[1024]{0:T(1024)S(1)} %broadcast_clamp_fusion), kind=kCustom, calls=%fused_computation | custom fusion | bytes 8392704 | tf_op jit(solution)/shard_map/gather | solution.py:126
  1033.6 6.6 fusion
  1040.2 0.9 fusion.20
  (37 shorter events, 0.9 us)
Async XLA Ops:
  7.2 875.5 %copy-start = (bf16[1,768,2048]{2,1,0:T(8,128)(2,1)S(1)}, bf16[1,768,2048]{2,1,0:T(8,128)(2,1)}, u32[]{:S(2)}) copy-start(bf16[1,768,2048]{2,1,0:T(8,128)(2,1)} %param.21) | copy-start | bytes 9437188
  7.2 702.3 %all-gather.2.cloned.1.call-start = ((), (), s32[]{:S(2)}) async-start(), calls=%async_computation.2 | async-start | bytes 8421376 | tf_op jit(solution)/shard_map/all_gather | solution.py:91
  10.0 19.3 %copy-start.4 = (f32[128,16]{0,1:T(8,128)S(1)}, f32[128,16]{0,1:T(8,128)}, u32[]{:S(2)}) copy-start(f32[128,16]{0,1:T(8,128)} %param.16) | copy-start | bytes 24580
  10.7 11.6 %collective-permute-start = (bf16[2,128,256]{1,2,0:T(8,128)(2,1)}, bf16[2,128,256]{1,2,0:T(8,128)(2,1)}, u32[]{:S(2)}, u32[]{:S(2)}) collective-permute-start(bf16[2,128,256]{1,2,0:T(8,128)(2,1)} %pad_maximum_fusion), channel_id=1, source_target_pairs={{0,32},{32,64},{64,96},{96,128},{128,160},{160,192},{192,224},{224... | collective-permute-start | bytes 393224 | tf_op jit(solution)/shard_map/ppermute | solution.py:15
  22.3 5.4 collective-permute-start.1
  26.7 3.0 copy-start.3
  709.4 5.7 copy-start.5
  714.3 0.8 copy-start.1
  888.8 8.2 copy-start.6
  888.8 132.7 %all-to-all-start.1 = ((bf16[32,40,2048]{2,1,0:T(8,128)(2,1)}), bf16[32,40,2048]{2,1,0:T(8,128)(2,1)}, u32[]{:S(2)}, u32[]{:S(2)}) async-start(bf16[32,40,2048]{2,1,0:T(8,128)(2,1)} %bitcast.80), calls=%async_computation.1 | async-start | bytes 10485760 | tf_op jit(solution)/shard_map/all_to_all | solution.py:125
  1033.6 6.6 copy-start.2
Sparse Core Ops, SparseCore 0:
  9.9 699.5 all-gather.1
where the time goes:
time: 1050 us
  waiting for transfers between devices  801 us (76%)
  blocking collectives  146 us (14%)
  local copies, waits for them, and re-layouts  33.8 us (3%)
  matrix products  24.4 us (2%)
  other arithmetic  19.7 us (2%)
  between operations  14.3 us (1%)
    all_gather x1, waiting for transfers between devices, shards(): lax.all_gather(out_proj, ('ctx', 'ep'), axis=0, tiled=True)  678 us
    all_to_all x1, blocking collectives, shards(): lax.all_to_all(outgoing, 'ep', split_axis=0, concat_axis=0, tiled=True)  146 us
    all_to_all x1, waiting for transfers between devices, shards(): lax.all_to_all(replies, 'ep', split_axis=0, concat_axis=0, tiled=True)  122 us
  transfers between devices with their start and end apart: 4, of which 2 were waited for; matrix products, arithmetic and copies ran while one was open for 2% of the time, Pallas kernels for 0%

commit v1 on v0

--- a/solution.py
+++ b/solution.py
@@ -88,7 +88,12 @@
     model_width = out_proj.shape[1]
     projected = jnp.dot(
         attended,
-        lax.all_gather(out_proj, ("ctx", "ep"), axis=0, tiled=True),
+        jnp.concatenate(
+            lax.all_to_all(
+                jnp.stack([out_proj] * lax.axis_size(("ctx", "ep"))), ("ctx", "ep"), 0, 0
+            ),
+            axis=0,
+        ),
         preferred_element_type=jnp.float32,
     )
     mixed_state = (residual.astype(jnp.float32) + projected).astype(jnp.bfloat16)

time: 1050 us -> 533 us (0.51)
  waiting for transfers between devices: 801 us -> 293 us
  starting transfers between devices: 8.32 us -> 26.3 us
  blocking collectives: 146 us -> 132 us
  between operations: 14.3 us -> 0.9 us
    all_gather x1 -> x0, waiting for transfers between devices: 678 us -> none  [shards(): lax.all_gather(out_proj, ('ctx', 'ep'), axis=0, tiled=True)]
    ppermute x2, waiting for transfers between devices: 0.01 us -> 166 us  [passed_along(): lax.ppermute(shard, axis, [(i, (i + by) % devices) for i in range(devices)])]
    all_to_all x0 -> x1, starting transfers between devices: none -> 15.3 us  [shards(): lax.all_to_all(jnp.stack([out_proj] * lax.axis_size(('ctx', 'ep'))), ('ct...]
    all_to_all x1, blocking collectives: 146 us -> 132 us  [shards(): lax.all_to_all(outgoing, 'ep', split_axis=0, concat_axis=0, tiled=True)]
  transfers between devices with their start and end apart: 4 -> 4, of which waited for: 2 -> 2; matrix products, arithmetic and copies ran while one was open for 2% -> 4% of each run, Pallas kernels for 0% -> 0%
where the time goes in v1:
time: 533 us; the launch traced here: 532 us
  waiting for transfers between devices  293 us (55%)
  blocking collectives  132 us (25%)
  local copies, waits for them, and re-layouts  36.4 us (7%)
  starting transfers between devices  26.3 us (5%)
  matrix products  24.4 us (5%)
  other arithmetic  19 us (4%)
    ppermute x2, waiting for transfers between devices, passed_along(): lax.ppermute(shard, axis, [(i, (i + by) % devices) for i in range(devices)])  166 us
    all_to_all x1, blocking collectives, shards(): lax.all_to_all(outgoing, 'ep', split_axis=0, concat_axis=0, tiled=True)  132 us
    all_to_all x1, waiting for transfers between devices, shards(): lax.all_to_all(replies, 'ep', split_axis=0, concat_axis=0, tiled=True)  126 us
    all_to_all x1, starting transfers between devices, shards(): lax.all_to_all(jnp.stack([out_proj] * lax.axis_size(('ctx', 'ep'))), ('ct...  15.3 us
    gather x1, local copies, waits for them, and re-layouts, shards(): returned.reshape(experts_all * capacity, model_width)[slot_ids]  12 us
  transfers between devices with their start and end apart: 4, of which 2 were waited for; matrix products, arithmetic and copies ran while one was open for 4% of the time, Pallas kernels for 0%

profile of v1, /device:TPU:105, one launch (start us, length us, event | category | flops | bytes accessed | tf_op | source)
XLA Modules:
  0.0 531.7 jit_solution(3390048454638357686)
XLA Ops:
  0.6 5.2 stack.11
  5.8 15.3 %all-to-all-start = ((bf16[256,8,2048]{2,1,0:T(8,128)(2,1)}), bf16[256,8,2048]{2,1,0:T(8,128)(2,1)}, u32[]{:S(2)}, u32[]{:S(2)}) async-start(bf16[256,8,2048]{2,1,0:T(8,128)(2,1)} %stack.11), calls=%async_computation | async-start | bytes 16777216 | tf_op jit(solution)/shard_map/all_to_all | solution.py:92
  21.1 0.1 copy.21
  21.3 0.1 copy.22
  21.4 0.7 pad_maximum_fusion
  22.3 9.0 %reduce-window.6 = s32[32,8,128]{2,1,0:T(8,128)S(1)} reduce-window(s32[32,8,128]{2,1,0:T(8,128)S(1)} %fusion.36, s32[]{:T(128)} %constant.58.clone.1), window={size=1x1x128 pad=0_0x0_0x127_0}, to_apply=%region_2.3 | reduce-window | flops 4161536 | bytes 262148 | tf_op jit(solution)/shard_map/reduce-window
  31.4 0.1 copy.30
  31.7 0.1 fusion.34
  32.0 0.1 copy.27
  32.3 166.3 %collective-permute-done = bf16[2,128,256]{1,2,0:T(8,128)(2,1)} collective-permute-done((bf16[2,128,256]{1,2,0:T(8,128)(2,1)}, bf16[2,128,256]{1,2,0:T(8,128)(2,1)}, u32[]{:S(2)}, u32[]{:S(2)}) %collective-permute-start) | collective-permute-done | bytes 131104 | tf_op jit(solution)/shard_map/ppermute | solution.py:15
  198.6 4.3 collective-permute-start.1
  202.9 2.0 copy.38
  204.8 2.2 copy.20
  207.1 1.0 constant_dynamic-update-slice_fusion.1
  208.2 1.6 fusion.46
  209.8 0.3 fusion.19
  210.1 1.3 fusion.23
  211.4 4.9 fusion.13
  216.3 0.2 fusion.24
  216.5 0.6 copy-done.1
  217.1 1.0 fusion.26
  218.1 10.1 %scatter_custom_fusion = bf16[1280,2048]{1,0:T(8,128)(2,1)} fusion(s32[1024]{0:T(1024)S(1)} %bitcast.100, bf16[]{:T(256)} %constant.69.clone.1, bf16[128,2048]{1,0:T(8,128)(2,1)} %fusion.26), kind=kCustom, calls=%fused_computation.9 | custom fusion | bytes 5767170 | tf_op jit(solution)/shard_map/scatter | solution.py:118
  228.2 132.1 %all_to_all.15 = bf16[32,40,2048]{2,1,0:T(8,128)(2,1)S(1)} all-to-all(bf16[32,40,2048]{2,1,0:T(8,128)(2,1)} %bitcast.85), channel_id=1, replica_groups=mesh['ctx'=8,'ep'=32] {'ep'}, dimensions={0} | all-to-all | bytes 10485760 | tf_op jit(solution)/shard_map/all_to_all | solution.py:125
  360.3 10.5 %fusion.3 = f32[1280,1536]{1,0:T(8,128)S(1)} fusion(bf16[1280,2048]{1,0:T(8,128)(2,1)S(1)} %bitcast.87, bf16[1,2048,1536]{2,1,0:T(8,128)(2,1)} %param.20), kind=kOutput, calls=%fused_computation.7 | convolution fusion | flops 8053063680 | bytes 19398656 | tf_op jit(solution)/shard_map/dot_general | solution.py:20
  370.8 6.1 %convolution_convert_fusion = bf16[1280,2048]{1,0:T(8,128)(2,1)} fusion(bf16[1,768,2048]{2,1,0:T(8,128)(2,1)S(1)} %copy-done, f32[1280,1536]{1,0:T(8,128)S(1)} %fusion.3), kind=kOutput, calls=%fused_computation.6 | convolution fusion | flops 4035051520 | bytes 16252928 | tf_op jit(solution)/shard_map/dot_general | solution.py:24
  376.9 6.7 %all-to-all-start.2 = ((bf16[32,40,2048]{2,1,0:T(8,128)(2,1)}), bf16[32,40,2048]{2,1,0:T(8,128)(2,1)}, u32[]{:S(2)}, u32[]{:S(2)}) async-start(bf16[32,40,2048]{2,1,0:T(8,128)(2,1)} %bitcast.86), calls=%async_computation.2 | async-start | bytes 10485760 | tf_op jit(solution)/shard_map/all_to_all | solution.py:130
  383.6 0.1 copy.26
  383.7 2.0 copy.32
  385.8 126.4 %all-to-all-done.2 = bf16[32,40,2048]{2,1,0:T(8,128)(2,1)} async-done(((bf16[32,40,2048]{2,1,0:T(8,128)(2,1)}), bf16[32,40,2048]{2,1,0:T(8,128)(2,1)}, u32[]{:S(2)}, u32[]{:S(2)}) %all-to-all-start.2) | async-done | bytes 5242912 | tf_op jit(solution)/shard_map/all_to_all | solution.py:130
  512.2 12.0 %gather_fusion = bf16[1024,2048]{1,0:T(8,128)(2,1)} fusion(bf16[1280,2048]{1,0:T(8,128)(2,1)} %bitcast.26, s32[1024]{0:T(1024)S(1)} %broadcast_clamp_fusion), kind=kCustom, calls=%fused_computation | custom fusion | bytes 8392704 | tf_op jit(solution)/shard_map/gather | solution.py:131
  524.2 6.6 %fusion = f32[128,2048]{1,0:T(8,128)S(1)} fusion(bf16[1024,2048]{1,0:T(8,128)(2,1)} %gather_fusion, f32[128,8]{1,0:T(8,128)S(1)} %copy.26), kind=kLoop, calls=%fused_computation.3 | loop fusion | flops 6029312 | bytes 5246976 | tf_op jit(solution)/shard_map/reduce_sum | solution.py:134
  530.8 0.9 fusion.27
  (43 shorter events, 0.9 us)
Async XLA Ops:
  0.6 370.2 %copy-start = (bf16[1,768,2048]{2,1,0:T(8,128)(2,1)S(1)}, bf16[1,768,2048]{2,1,0:T(8,128)(2,1)}, u32[]{:S(2)}) copy-start(bf16[1,768,2048]{2,1,0:T(8,128)(2,1)} %param.21) | copy-start | bytes 9437188
  5.8 15.3 %copy-start.4 = (bf16[128,256]{1,0:T(8,128)(2,1)S(1)}, bf16[128,256]{1,0:T(8,128)(2,1)}, u32[]{:S(2)}) copy-start(bf16[128,256]{1,0:T(8,128)(2,1)} %param.13) | copy-start | bytes 196612
  5.8 15.4 %copy-start.5 = (bf16[128,256]{1,0:T(8,128)(2,1)S(1)}, bf16[128,256]{1,0:T(8,128)(2,1)}, u32[]{:S(2)}) copy-start(bf16[128,256]{1,0:T(8,128)(2,1)} %param.14) | copy-start | bytes 196612
  5.8 16.2 %copy-start.7 = (s32[128,8]{0,1:T(8,128)S(1)}, s32[128,8]{0,1:T(8,128)}, u32[]{:S(2)}) copy-start(s32[128,8]{0,1:T(8,128)} %param.22) | copy-start | bytes 12292
  5.8 205.6 %all-to-all-start = ((bf16[256,8,2048]{2,1,0:T(8,128)(2,1)}), bf16[256,8,2048]{2,1,0:T(8,128)(2,1)}, u32[]{:S(2)}, u32[]{:S(2)}) async-start(bf16[256,8,2048]{2,1,0:T(8,128)(2,1)} %stack.11), calls=%async_computation | async-start | bytes 16777216 | tf_op jit(solution)/shard_map/all_to_all | solution.py:92
  21.4 188.4 %copy-start.6 = (f32[128,16]{0,1:T(8,128)S(1)}, f32[128,16]{0,1:T(8,128)}, u32[]{:S(2)}) copy-start(f32[128,16]{0,1:T(8,128)} %param.16) | copy-start | bytes 24580
  22.1 176.5 %collective-permute-start = (bf16[2,128,256]{1,2,0:T(8,128)(2,1)}, bf16[2,128,256]{1,2,0:T(8,128)(2,1)}, u32[]{:S(2)}, u32[]{:S(2)}) collective-permute-start(bf16[2,128,256]{1,2,0:T(8,128)(2,1)} %pad_maximum_fusion), channel_id=1, source_target_pairs={{0,32},{32,64},{64,96},{96,128},{128,160},{160,192},{192,224},{224... | collective-permute-start | bytes 393224 | tf_op jit(solution)/shard_map/ppermute | solution.py:15
  198.6 9.5 %collective-permute-start.1 = (bf16[2,128,256]{1,2,0:T(8,128)(2,1)}, bf16[2,128,256]{1,2,0:T(8,128)(2,1)S(1)}, u32[]{:S(2)}, u32[]{:S(2)}) collective-permute-start(bf16[2,128,256]{1,2,0:T(8,128)(2,1)} %collective-permute-done), channel_id=1, source_target_pairs={{0,32},{32,64},{64,96},{96,128},{128,160},{160,192},{192,224},{224... | collective-permute-start | bytes 393224 | tf_op jit(solution)/shard_map/ppermute | solution.py:15
  207.1 3.0 copy-start.3
  211.4 5.7 %copy-start.8 = (f32[2048]{0:T(1024)S(1)}, f32[2048]{0:T(1024)}, u32[]{:S(2)}) copy-start(f32[2048]{0:T(1024)} %param.19) | copy-start | bytes 24580
  216.3 0.8 copy-start.1
  376.9 6.7 %copy-start.9 = (f32[128,8]{0,1:T(8,128)S(1)}, f32[128,8]{0,1:T(8,128)}, u32[]{:S(2)}) copy-start(f32[128,8]{0,1:T(8,128)} %param.23) | copy-start | bytes 12292
  376.9 135.3 %all-to-all-start.2 = ((bf16[32,40,2048]{2,1,0:T(8,128)(2,1)}), bf16[32,40,2048]{2,1,0:T(8,128)(2,1)}, u32[]{:S(2)}, u32[]{:S(2)}) async-start(bf16[32,40,2048]{2,1,0:T(8,128)(2,1)} %bitcast.86), calls=%async_computation.2 | async-start | bytes 10485760 | tf_op jit(solution)/shard_map/all_to_all | solution.py:130
  524.2 6.6 %copy-start.2 = (bf16[128,2048]{1,0:T(8,128)(2,1)S(1)}, bf16[128,2048]{1,0:T(8,128)(2,1)}, u32[]{:S(2)}) copy-start(bf16[128,2048]{1,0:T(8,128)(2,1)} %copy-done.1) | copy-start | bytes 1572868
